TPU v7x, 1024 devices: a whole 8x8x8 slice. The times are simulated.
1024 devices in a mesh: expert: 64 (over x, y_lo, core), section: 8 (over z), tensor: 2 (over y_hi).
Axes of the slice: x: 8, y: 8 (y_hi: 2, y_lo: 4; y = y_hi * 4 + y_lo), z: 8, core: 2. Of those that a mesh axis runs over, the one named last changes fastest.
Arguments:
- tokens: bfloat16 [2048, 7168], P(('expert', 'tensor')), may hold values from -6 to 6
- norm_gain: float32 [7168], replicated, may hold values from 0.1 to 1.9
- expert_ids: int32 [2048, 8], P(('expert', 'tensor')), may hold values from 0 to 63, all different within a row; in each aligned block of 16 rows (0 to 15, 16 to 31, ...) at most 3 rows name the same one
- route_weights: float32 [2048, 8], P(('expert', 'tensor')), may hold values from 0.05 to 1
- gate_weight: bfloat16 [64, 7168, 1024], P('expert', 'tensor', 'section'), may hold values from -0.0625 to 0.0625
- up_weight: bfloat16 [64, 7168, 1024], P('expert', 'tensor', 'section'), may hold values from -0.0625 to 0.0625
- down_weight: bfloat16 [64, 7168, 1024], P('expert', 'tensor', 'section'), may hold values from -0.1875 to 0.1875
- queries: bfloat16 [1024, 128, 576], P(('expert', 'tensor'), 'section'), may hold values from -300 to 300
- kv_cache: bfloat16 [1024, 384, 576], P(('expert', 'tensor')), may hold values from -8 to 8
- cache_lengths: int32 [1024], P(('expert', 'tensor')), may hold values from 2 to 384
Outputs:
- moe_out: bfloat16 [2048, 7168], P(('expert', 'tensor'), 'section')
- attn_out: bfloat16 [1024, 128, 512], P(('expert', 'tensor'), 'section')
Inputs may be any that keep to these rules, and one draw needn't show every extreme that they name: `expert_ids`: each row names 8 different experts; among the 16 rows of one device no expert is named more than 3 times, and on some device some expert is named exactly 3 times.
All inputs are finite; a program needn't handle non-finite values.
Results may differ from a plain program's by a relative error of at most 0.006.
Values may be sent and summed in bfloat16 or wider, within the bound.
No kernel may reach another device: no remote copies, remote signals or barrier semaphores. Data moves between devices by JAX's collectives and lax.ppermute only.
A program may use at most 64 MiB of HBM per device.

v0:
```python
import jax
import jax.numpy as jnp
from jax import lax
from jax.sharding import Mesh
from jax.sharding import PartitionSpec as P

LAT = 512
EXPERT = ("expert_0", "expert_1", "expert_2")
EXPERT_TENSOR = ("expert_0", "expert_1", "expert_2", "tensor")


norm_eps = 1e-06
score_scale = 192.0 ** (-0.5)


def sent_together(arrays, axis, dim, along):
    ends, at = ([], 0)
    for a in arrays[:-1]:
        at += a.shape[along]
        ends.append(at)
    both = jnp.concatenate(arrays, axis=along)
    return tuple(jnp.split(lax.all_gather(both, axis, axis=dim, tiled=True), ends, axis=along))


def split_up(shard, dim, count):
    before, after = (shard.shape[:dim], shard.shape[dim + 1 :])
    return jnp.moveaxis(shard.reshape(*before, count, -1, *after), dim, 0)


def in_order(parts, dim):
    parts = jnp.moveaxis(parts, 0, dim)
    shape = parts.shape
    return parts.reshape(*shape[:dim], shape[dim] * shape[dim + 1], *shape[dim + 2 :])


def moved_by_axis(parts, axes, sequence):
    inside = parts.shape[1:]
    whole = parts.reshape(*(lax.axis_size(a) for a in axes), *inside)
    for k in sequence:
        whole = lax.all_to_all(whole, axes[k], k, k, tiled=True)
    return whole.reshape(-1, *inside)


def two_step_exchange(shard, groups, sequence, split_dim, concat_dim):
    count = lax.axis_size(groups[0]) * lax.axis_size(groups[1])
    parts = split_up(shard, split_dim, count)
    return in_order(moved_by_axis(parts, groups, sequence), concat_dim)


def from_everyone(shard, axis):
    copies = jnp.broadcast_to(shard, (lax.axis_size(axis), *shard.shape))
    return lax.all_to_all(copies, axis, split_axis=0, concat_axis=0, tiled=True)


def collect(shard, axis, dim):
    return in_order(from_everyone(shard, axis), dim)


def rms_rows(tokens, norm_gain):
    values = tokens.astype(jnp.float32)
    factor = lax.rsqrt(jnp.mean(values * values, axis=-1, keepdims=True) + norm_eps)
    return (values * factor * norm_gain).astype(jnp.bfloat16)


def attend(queries, kv_cache, cache_lengths):
    scores = (
        jnp.einsum("rhc,rlc->rhl", queries, kv_cache, preferred_element_type=jnp.float32)
        * score_scale
    )
    position = jnp.arange(kv_cache.shape[1], dtype=jnp.int32)
    is_live = position[None, None, :] < cache_lengths[:, None, None]
    scores = jnp.where(is_live, scores, -jnp.inf)
    top_score = jnp.max(scores, axis=-1, keepdims=True)
    powers = jnp.exp(scores - top_score)
    weights = (powers / jnp.sum(powers, axis=-1, keepdims=True)).astype(jnp.bfloat16)
    latents = kv_cache[:, :, :LAT]
    return jnp.einsum("rhl,rlc->rhc", weights, latents, preferred_element_type=jnp.float32).astype(
        jnp.bfloat16
    )


def per_device(
    tokens,
    norm_gain,
    expert_ids,
    route_weights,
    gate_weight,
    up_weight,
    down_weight,
    queries,
    kv_cache,
    cache_lengths,
):
    normed = rms_rows(tokens, norm_gain)
    experts = lax.axis_size(EXPERT)
    sections = lax.axis_size("section")
    row_count, top_count = expert_ids.shape
    capacity = max(2, row_count * top_count // experts + 1)
    slot_count = experts * capacity
    choose = (expert_ids[:, :, None] == jnp.arange(experts, dtype=jnp.int32)).astype(jnp.int32)
    flat_choose = choose.reshape(row_count * top_count, experts)
    earlier = jnp.cumsum(flat_choose, axis=0) - flat_choose
    ranking = jnp.sum(earlier * flat_choose, axis=1).reshape(row_count, top_count)
    slot_of = expert_ids * capacity + ranking
    matches = slot_of[:, :, None] == jnp.arange(slot_count, dtype=jnp.int32)
    placing = jnp.sum(matches.astype(jnp.float32), axis=1).astype(jnp.bfloat16)
    mixing = jnp.sum(jnp.where(matches, route_weights[:, :, None], 0.0), axis=1)
    packed = lax.dot_general(
        placing, normed, (((0,), (0,)), ((), ())), preferred_element_type=jnp.float32
    ).astype(jnp.bfloat16)
    gate_full, up_full, down_full = sent_together(
        (gate_weight[0], up_weight[0], down_weight[0]), "tensor", 0, 1
    )
    arrived = two_step_exchange(packed, (("expert_0", "expert_1"), "expert_2"), (1, 0), 0, 0)
    gate_sum = jnp.dot(arrived, gate_full, preferred_element_type=jnp.float32)
    up_sum = jnp.dot(arrived, up_full, preferred_element_type=jnp.float32)
    hidden = (jax.nn.silu(gate_sum) * up_sum).astype(jnp.bfloat16)
    down_cols = lax.all_to_all(down_full, "section", split_axis=0, concat_axis=1, tiled=True)
    expert_part = lax.dot_general(
        down_cols,
        collect(hidden, "section", 1),
        (((1,), (1,)), ((), ())),
        preferred_element_type=jnp.float32,
    ).astype(jnp.bfloat16)
    returned = lax.all_to_all(expert_part, EXPERT, split_axis=1, concat_axis=1, tiled=True)
    own_width = tokens.shape[1] // sections
    own_cols = lax.dynamic_slice_in_dim(
        tokens, lax.axis_index("section") * own_width, own_width, 1
    ).astype(jnp.float32)
    mixed = own_cols + lax.dot_general(
        mixing, returned.astype(jnp.float32), (((1,), (1,)), ((), ()))
    )
    moe_out = mixed.astype(jnp.bfloat16)
    attn_out = attend(queries, kv_cache, cache_lengths)
    return (moe_out, attn_out)


def solution(mesh):
    torus = Mesh(
        mesh.devices.reshape(8, 4, 2, mesh.shape["section"], mesh.shape["tensor"]),
        ("expert_0", "expert_1", "expert_2", "section", "tensor"),
    )
    return jax.shard_map(
        per_device,
        mesh=torus,
        in_specs=(
            P(EXPERT_TENSOR, None),
            P(),
            P(EXPERT_TENSOR, None),
            P(EXPERT_TENSOR, None),
            P(EXPERT, "tensor", "section"),
            P(EXPERT, "tensor", "section"),
            P(EXPERT, "tensor", "section"),
            P(EXPERT_TENSOR, "section", None),
            P(EXPERT_TENSOR, None, None),
            P(EXPERT_TENSOR),
        ),
        out_specs=(P(EXPERT_TENSOR, "section"), P(EXPERT_TENSOR, "section", None)),
        check_vma=False,
    )
```

profile of v0, /device:TPU:112, one launch (start us, length us, event | category | flops | bytes accessed | tf_op | source)
XLA Modules:
  0.0 344.6 jit_solution(11603105599795883251)
XLA Ops:
  7.2 3.6 %pad_maximum_fusion = bf16[3584,384]{1,0:T(8,128)(2,1)} fusion(bf16[3584,128]{1,0:T(8,128)(2,1)} %bitcast.31, bf16[3584,128]{1,0:T(8,128)(2,1)} %bitcast.32, bf16[3584,128]{1,0:T(8,128)(2,1)} %bitcast.33), kind=kLoop, calls=%fused_computation.4 | loop fusion | flops 8257536 | bytes 5505024 | tf_op jit(solution)/shard_map/concatenate | solution.py:21
  10.9 0.6 copy-done.3
  11.7 0.1 fusion.36
  11.8 0.2 reduce_window_sum.11
  12.0 0.2 select_reduce_fusion.1
  12.3 0.2 fusion.28
  12.5 0.2 convert_reduce_fusion
  12.7 0.9 convolution_convert_fusion
  13.6 4.2 %reshape_reshape.6 = bf16[32,2,3,7168]{3,2,1,0:T(4,128)(2,1)} reshape(bf16[192,7168]{1,0:T(8,128)(2,1)S(1)} %convolution_convert_fusion) | data formatting | bytes 5505024 | tf_op jit(solution)/shard_map/reshape;reshape | solution.py:38
  17.9 4.0 %copy.30 = bf16[32,2,3,7168]{3,0,2,1:T(8,128)(2,1)S(1)} copy(bf16[32,2,3,7168]{3,2,1,0:T(4,128)(2,1)} %reshape_reshape.6) | data formatting | bytes 5505024 | tf_op jit(solution)/shard_map/reshape;reshape | solution.py:38
  21.9 5.9 %all_to_all.43 = bf16[32,2,3,7168]{3,0,2,1:T(8,128)(2,1)S(1)} all-to-all(bf16[32,2,3,7168]{3,0,2,1:T(8,128)(2,1)S(1)} %copy.30), channel_id=1, replica_groups=mesh['expert_0'=8,'expert_1'=4,'expert_2'=2,'section'=8,'tensor'=2] {'ex..., dimensions={1} | all-to-all | bytes 5505024 | tf_op jit(solution)/shard_map/all_to_all | solution.py:40
  27.8 2.8 copy.31
  30.7 188.0 %all_to_all.44 = bf16[32,2,3,7168]{3,1,2,0:T(2,128)(2,1)S(1)} all-to-all(bf16[32,2,3,7168]{3,1,2,0:T(2,128)(2,1)S(1)} %copy.31), channel_id=1, replica_groups=mesh['expert_0'=8,'expert_1'=4,'expert_2'=2,'section'=8,'tensor'=2] {'ex..., dimensions={0} | all-to-all | bytes 5505024 | tf_op jit(solution)/shard_map/all_to_all | solution.py:40
  218.7 3.7 %copy.32 = bf16[32,2,3,7168]{3,2,1,0:T(4,128)(2,1)} copy(bf16[32,2,3,7168]{3,1,2,0:T(2,128)(2,1)S(1)} %all_to_all.44) | data formatting | bytes 5505024 | tf_op jit(solution)/shard_map/all_to_all | solution.py:40
  222.4 5.7 %reshape_reshape.7 = bf16[192,7168]{1,0:T(8,128)(2,1)S(1)} reshape(bf16[32,2,3,7168]{3,2,1,0:T(4,128)(2,1)} %copy.32) | data formatting | bytes 5505024 | tf_op jit(solution)/shard_map/reshape;reshape | solution.py:33
  228.1 2.4 fusion.5
  230.5 2.4 fusion.24
  232.9 0.8 broadcast_in_dim.40
  233.7 11.9 %all-to-all-start.3 = ((bf16[8,192,128]{2,1,0:T(8,128)(2,1)}), bf16[8,192,128]{2,1,0:T(8,128)(2,1)S(1)}, u32[]{:S(2)}, u32[]{:S(2)}) async-start(bf16[8,192,128]{2,1,0:T(8,128)(2,1)} %broadcast_in_dim.40), calls=%async_computation.3 | async-start | bytes 786432 | tf_op jit(solution)/shard_map/all_to_all | solution.py:52
  245.6 2.9 split.12
  248.5 11.5 %all-to-all-done.3 = bf16[8,192,128]{2,1,0:T(8,128)(2,1)S(1)} async-done(((bf16[8,192,128]{2,1,0:T(8,128)(2,1)}), bf16[8,192,128]{2,1,0:T(8,128)(2,1)S(1)}, u32[]{:S(2)}, u32[]{:S(2)}) %all-to-all-start.3) | async-done | bytes 393248 | tf_op jit(solution)/shard_map/all_to_all | solution.py:52
  260.0 3.8 %all-to-all-start = ((bf16[8,896,128]{2,1,0:T(8,128)(2,1)}), bf16[8,896,128]{2,1,0:T(8,128)(2,1)S(1)}, u32[]{:S(2)}, u32[]{:S(2)}) async-start(bf16[8,896,128]{2,1,0:T(8,128)(2,1)} %bitcast.3), calls=%async_computation | async-start | bytes 3670016 | tf_op jit(solution)/shard_map/all_to_all | solution.py:118
  263.9 44.1 %all-to-all-done = bf16[8,896,128]{2,1,0:T(8,128)(2,1)S(1)} async-done(((bf16[8,896,128]{2,1,0:T(8,128)(2,1)}), bf16[8,896,128]{2,1,0:T(8,128)(2,1)S(1)}, u32[]{:S(2)}, u32[]{:S(2)}) %all-to-all-start) | async-done | bytes 1835040 | tf_op jit(solution)/shard_map/all_to_all | solution.py:118
  308.0 0.8 fusion.12
  308.7 0.9 all_to_all.35
  309.7 10.8 %all-to-all-start.4 = ((bf16[896,64,3]{0,2,1:T(4,128)(2,1)}), bf16[896,64,3]{0,2,1:T(4,128)(2,1)S(1)}, u32[]{:S(2)}, u32[]{:S(2)}) async-start(bf16[896,64,3]{0,2,1:T(4,128)(2,1)} %all_to_all.35), calls=%async_computation.4 | async-start | bytes 917504 | tf_op jit(solution)/shard_map/all_to_all | solution.py:125
  320.5 2.6 fusion.16
  323.1 0.2 fusion.39
  323.3 3.5 %fusion.18 = bf16[8,16,512]{2,1,0:T(8,128)(2,1)} fusion(bf16[8,384,576]{1,2,0:T(8,128)(2,1)} %param.18, f32[8,16]{1,0:T(8,128)S(1)} %fusion.39, f32[8,16,384]{2,1,0:T(8,128)S(1)} %fusion.16), kind=kOutput, calls=%fused_computation.17 | convolution fusion | flops 50545152 | bytes 3674112 | tf_op jit(solution)/shard_map/rhl,rlc->rhc/dot_general | solution.py:77
  326.8 9.8 %all-to-all-done.4 = bf16[896,64,3]{0,2,1:T(4,128)(2,1)S(1)} async-done(((bf16[896,64,3]{0,2,1:T(4,128)(2,1)}), bf16[896,64,3]{0,2,1:T(4,128)(2,1)S(1)}, u32[]{:S(2)}, u32[]{:S(2)}) %all-to-all-start.4) | async-done | bytes 344096 | tf_op jit(solution)/shard_map/all_to_all | solution.py:125
  336.7 0.3 all_to_all.37
  337.0 0.8 fusion.27
  (21 shorter events, 0.5 us)
Async XLA Ops:
  7.2 313.4 %copy-start = (bf16[8,16,576]{2,1,0:T(8,128)(2,1)S(1)}, bf16[8,16,576]{2,1,0:T(8,128)(2,1)}, u32[]{:S(2)}) copy-start(bf16[8,16,576]{2,1,0:T(8,128)(2,1)} %param.17) | copy-start | bytes 442372
  7.2 220.9 %all-gather.2.cloned.1.call-start = ((), (), s32[]{:S(2)}) async-start(), calls=%async_computation.5 | async-start | bytes 8257536 | tf_op jit(solution)/shard_map/all_gather | solution.py:22
  10.9 0.7 copy-start.3
  10.9 1.4 copy-start.4
  10.9 1.5 copy-start.1
  10.9 1.8 copy-start.2
  233.7 26.3 %all-to-all-start.3 = ((bf16[8,192,128]{2,1,0:T(8,128)(2,1)}), bf16[8,192,128]{2,1,0:T(8,128)(2,1)S(1)}, u32[]{:S(2)}, u32[]{:S(2)}) async-start(bf16[8,192,128]{2,1,0:T(8,128)(2,1)} %broadcast_in_dim.40), calls=%async_computation.3 | async-start | bytes 786432 | tf_op jit(solution)/shard_map/all_to_all | solution.py:52
  248.5 15.3 %copy-start.5 = (s32[8]{0:T(128)S(1)}, s32[8]{0:T(128)}, u32[]{:S(2)}) copy-start(s32[8]{0:T(128)} %param.19) | copy-start | bytes 100
  260.0 48.0 %all-to-all-start = ((bf16[8,896,128]{2,1,0:T(8,128)(2,1)}), bf16[8,896,128]{2,1,0:T(8,128)(2,1)S(1)}, u32[]{:S(2)}, u32[]{:S(2)}) async-start(bf16[8,896,128]{2,1,0:T(8,128)(2,1)} %bitcast.3), calls=%async_computation | async-start | bytes 3670016 | tf_op jit(solution)/shard_map/all_to_all | solution.py:118
  309.7 27.0 %all-to-all-start.4 = ((bf16[896,64,3]{0,2,1:T(4,128)(2,1)}), bf16[896,64,3]{0,2,1:T(4,128)(2,1)S(1)}, u32[]{:S(2)}, u32[]{:S(2)}) async-start(bf16[896,64,3]{0,2,1:T(4,128)(2,1)} %all_to_all.35), calls=%async_computation.4 | async-start | bytes 917504 | tf_op jit(solution)/shard_map/all_to_all | solution.py:125
Sparse Core Ops, SparseCore 0:
  11.0 209.9 all-gather.1
where the time goes:
time: 345 us
  blocking collectives  194 us (56%)
  waiting for transfers between devices  65.5 us (19%)
  starting transfers between devices  26.6 us (8%)
  local copies, waits for them, and re-layouts  26.4 us (8%)
  between operations  14.2 us (4%)
  matrix products  13.3 us (4%)
  other arithmetic  4.71 us (1%)
    all_to_all x2, blocking collectives, moved_by_axis(): whole = lax.all_to_all(whole, axes[k], k, k, tiled=True)  194 us
    all_to_all x1, waiting for transfers between devices, per_device(): lax.all_to_all(down_full, 'section', split_axis=0, concat_axis=1, tiled=T...  44.1 us
    all_to_all x1, starting transfers between devices, from_everyone(): return lax.all_to_all(copies, axis, split_axis=0, concat_axis=0, tiled=True)  11.9 us
    all_to_all x1, waiting for transfers between devices, from_everyone(): return lax.all_to_all(copies, axis, split_axis=0, concat_axis=0, tiled=True)  11.5 us
    all_to_all x1, starting transfers between devices, per_device(): lax.all_to_all(expert_part, EXPERT, split_axis=1, concat_axis=1, tiled=True)  10.8 us
    all_to_all x1, waiting for transfers between devices, per_device(): lax.all_to_all(expert_part, EXPERT, split_axis=1, concat_axis=1, tiled=True)  9.83 us
    another operation x2, local copies, waits for them, and re-layouts, moved_by_axis(): whole = parts.reshape(*(lax.axis_size(a) for a in axes), *inside)  8.24 us
  transfers between devices with their start and end apart: 4, of which 3 were waited for; matrix products, arithmetic and copies ran while one was open for 9% of the time, Pallas kernels for 0%

commit v1 on v0

v1 whole, which is shorter than its diff:
```python
import jax
import jax.numpy as jnp
from jax import lax
from jax.sharding import Mesh
from jax.sharding import PartitionSpec as P

LAT = 512
CAP = 3
EXPERT = ("expert_0", "expert_1", "expert_2")
EXPERT_TENSOR = ("expert_0", "expert_1", "expert_2", "tensor")


norm_eps = 1e-06
score_scale = 192.0 ** (-0.5)


def rms_rows(tokens, norm_gain):
    values = tokens.astype(jnp.float32)
    factor = lax.rsqrt(jnp.mean(values * values, axis=-1, keepdims=True) + norm_eps)
    return (values * factor * norm_gain).astype(jnp.bfloat16)


def attend(queries, kv_cache, cache_lengths):
    scores = (
        jnp.einsum("rhc,rlc->rhl", queries, kv_cache, preferred_element_type=jnp.float32)
        * score_scale
    )
    position = jnp.arange(kv_cache.shape[1], dtype=jnp.int32)
    is_live = position[None, None, :] < cache_lengths[:, None, None]
    scores = jnp.where(is_live, scores, -jnp.inf)
    top_score = jnp.max(scores, axis=-1, keepdims=True)
    powers = jnp.exp(scores - top_score)
    weights = (powers / jnp.sum(powers, axis=-1, keepdims=True)).astype(jnp.bfloat16)
    latents = kv_cache[:, :, :LAT]
    return jnp.einsum("rhl,rlc->rhc", weights, latents, preferred_element_type=jnp.float32).astype(
        jnp.bfloat16
    )


def swapped(value, axis, by):
    size = lax.axis_size(axis)
    return lax.ppermute(value, axis, [(i, i ^ by) for i in range(size)])


def per_device(
    tokens,
    norm_gain,
    expert_ids,
    route_weights,
    gate_weight,
    up_weight,
    down_weight,
    queries,
    kv_cache,
    cache_lengths,
):
    f32, bf16 = jnp.float32, jnp.bfloat16
    experts = lax.axis_size(EXPERT)
    sections = lax.axis_size("section")
    tensors = lax.axis_size("tensor")
    section = lax.axis_index("section")
    parity = section % 2
    upper = section // (sections // 2)
    rows, width = tokens.shape
    half, units = gate_weight.shape[1:]
    quarter = half // 2
    eighth = quarter // 2
    piece = half // sections

    halves = jnp.stack([gate_weight[0], up_weight[0]]).reshape(2, 2, quarter, units)
    kept = lax.dynamic_index_in_dim(halves, parity, 1, keepdims=False)
    given = lax.dynamic_index_in_dim(halves, 1 - parity, 1, keepdims=False)
    taken = swapped(given, "section", 1)
    down_parts = jnp.moveaxis(down_weight[0].reshape(sections // 2, 2, piece, units), 1, 0)
    down_cols = lax.all_to_all(
        down_parts.reshape(sections, piece, units), "section", 0, 0, tiled=True
    )

    normed = rms_rows(tokens, norm_gain)
    slot_count = experts * CAP
    choose = (expert_ids[:, :, None] == jnp.arange(experts, dtype=jnp.int32)).astype(f32)
    per_row = jnp.sum(choose, axis=1)
    before = (jnp.arange(rows)[:, None] > jnp.arange(rows)[None, :]).astype(f32)
    earlier = jnp.dot(before, per_row)
    slots = jnp.arange(slot_count, dtype=jnp.int32)
    ranking = jnp.sum(choose * earlier[:, None, :], axis=2).astype(jnp.int32)
    slot_of = expert_ids * CAP + ranking
    matches = slot_of[:, :, None] == slots
    placing = jnp.sum(matches.astype(f32), axis=1).astype(bf16)
    mixing = jnp.sum(jnp.where(matches, route_weights[:, :, None], 0.0), axis=1)
    own = lax.dynamic_index_in_dim(
        normed.reshape(rows, tensors, 2, quarter), parity, 2, keepdims=False
    )
    packed = lax.dot_general(
        placing, own.reshape(rows, tensors * quarter), (((0,), (0,)), ((), ())),
        preferred_element_type=f32,
    ).astype(bf16)
    packed = packed.reshape(experts, CAP, tensors, 2, eighth).transpose(0, 2, 3, 1, 4)
    arrived = lax.all_to_all(
        packed.reshape(experts * tensors, 2, CAP * eighth), EXPERT_TENSOR, 0, 0, tiled=True
    )
    sources = experts * tensors
    inputs = arrived.reshape(sources, 2, CAP, eighth).transpose(0, 2, 1, 3)
    inputs = inputs.reshape(sources * CAP, quarter)

    def partial(weights):
        both = jnp.concatenate([weights[0], weights[1]], axis=1)
        return jnp.dot(inputs, both, preferred_element_type=f32)

    theirs = partial(taken).astype(bf16)
    sums = partial(kept) + swapped(theirs, "section", 1).astype(f32)
    sums = sums + swapped(sums.astype(bf16), "tensor", 1).astype(f32)
    hidden = (jax.nn.silu(sums[:, :units]) * sums[:, units:]).astype(bf16)

    copies = jnp.broadcast_to(hidden, (sections, *hidden.shape))
    hidden_all = lax.all_to_all(copies, "section", 0, 0, tiled=True)
    expert_out = lax.dot_general(
        jnp.moveaxis(hidden_all, 0, 1).reshape(sources * CAP, sections * units),
        jnp.moveaxis(down_cols, 0, 1).reshape(piece, sections * units),
        (((1,), (1,)), ((), ())),
        preferred_element_type=f32,
    ).astype(bf16)
    returned = lax.all_to_all(
        expert_out.reshape(sources, CAP, piece), EXPERT_TENSOR, 0, 0, tiled=True
    )
    returned = returned.reshape(experts, tensors, CAP, piece).transpose(1, 0, 2, 3)
    returned = returned.reshape(tensors, slot_count, piece)
    mixed = jnp.einsum("rs,tsc->trc", mixing, returned.astype(f32))
    mine = lax.dynamic_index_in_dim(mixed, upper, 0, keepdims=False)
    other = lax.dynamic_index_in_dim(mixed, 1 - upper, 0, keepdims=False)
    got = swapped(other, "section", sections // 2)
    summed = jnp.where(
        upper == 0, jnp.concatenate([mine, got], axis=1), jnp.concatenate([got, mine], axis=1)
    )
    own_width = width // sections
    own_cols = lax.dynamic_slice_in_dim(tokens, section * own_width, own_width, 1)
    moe_out = (own_cols.astype(f32) + summed).astype(bf16)
    attn_out = attend(queries, kv_cache, cache_lengths)
    return (moe_out, attn_out)


def solution(mesh):
    experts = mesh.shape["expert"]
    torus = Mesh(
        mesh.devices.reshape(experts // 8, 4, 2, mesh.shape["section"], mesh.shape["tensor"]),
        ("expert_0", "expert_1", "expert_2", "section", "tensor"),
    )
    return jax.shard_map(
        per_device,
        mesh=torus,
        in_specs=(
            P(EXPERT_TENSOR, None),
            P(),
            P(EXPERT_TENSOR, None),
            P(EXPERT_TENSOR, None),
            P(EXPERT, "tensor", "section"),
            P(EXPERT, "tensor", "section"),
            P(EXPERT, "tensor", "section"),
            P(EXPERT_TENSOR, "section", None),
            P(EXPERT_TENSOR, None, None),
            P(EXPERT_TENSOR),
        ),
        out_specs=(P(EXPERT_TENSOR, "section"), P(EXPERT_TENSOR, "section", None)),
        check_vma=False,
    )
```

time: 345 us -> 195 us (0.57)
  the two profiles are of different devices: /device:TPU:112 before, /device:TPU:16 now
where the time goes in v1:
time: 195 us; the launch traced here: 194 us
  waiting for transfers between devices  75.9 us (39%)
  starting transfers between devices  49.4 us (25%)
  blocking collectives  29.9 us (15%)
  local copies, waits for them, and re-layouts  21.6 us (11%)
  matrix products  9.8 us (5%)
  other arithmetic  6.11 us (3%)
    all_to_all x1, waiting for transfers between devices, per_device(): lax.all_to_all(packed.reshape(experts * tensors, 2, CAP * eighth), EXPERT...  32.3 us
    all_to_all x1, blocking collectives, per_device(): hidden_all = lax.all_to_all(copies, 'section', 0, 0, tiled=True)  29.9 us
    ppermute x4, waiting for transfers between devices, swapped(): return lax.ppermute(value, axis, [(i, i ^ by) for i in range(size)])  25.6 us
    all_to_all x1, starting transfers between devices, per_device(): lax.all_to_all(packed.reshape(experts * tensors, 2, CAP * eighth), EXPERT...  18.2 us
    all_to_all x1, waiting for transfers between devices, per_device(): lax.all_to_all(expert_out.reshape(sources, CAP, piece), EXPERT_TENSOR, 0,...  18 us
    all_to_all x1, starting transfers between devices, per_device(): lax.all_to_all(down_parts.reshape(sections, piece, units), 'section', 0,...  12.7 us
    ppermute x4, starting transfers between devices, swapped(): return lax.ppermute(value, axis, [(i, i ^ by) for i in range(size)])  11.7 us
    all_to_all x1, starting transfers between devices, per_device(): lax.all_to_all(expert_out.reshape(sources, CAP, piece), EXPERT_TENSOR, 0,...  6.85 us
  transfers between devices with their start and end apart: 7, of which 5 were waited for; matrix products, arithmetic and copies ran while one was open for 11% of the time, Pallas kernels for 0%

profile of v1, /device:TPU:16, one launch (start us, length us, event | category | flops | bytes accessed | tf_op | source)
XLA Modules:
  0.0 193.7 jit_solution(1164706212035532407)
XLA Ops:
  0.7 1.1 fusion.19
  1.8 1.1 fusion.21
  3.1 0.8 dynamic-slice_reduce_fusion
  3.9 0.8 copy.43
  6.2 0.7 copy.63
  6.9 1.2 reshape.83
  8.1 2.5 %copy.47 = bf16[128,2,2688]{2,1,0:T(2,128)(2,1)} copy(bf16[128,2,2688]{2,0,1:T(8,128)(2,1)S(1)} %reshape.83) | data formatting | bytes 2752512 | tf_op jit(solution)/shard_map/reshape | solution.py:100
  10.6 18.2 %all-to-all-start = ((bf16[128,2,2688]{2,1,0:T(2,128)(2,1)}), bf16[128,2,2688]{2,1,0:T(2,128)(2,1)S(1)}, u32[]{:S(2)}, u32[]{:S(2)}) async-start(bf16[128,2,2688]{2,1,0:T(2,128)(2,1)} %copy.47), calls=%async_computation | async-start | bytes 2752512 | tf_op jit(solution)/shard_map/all_to_all | solution.py:99
  28.8 1.6 pad_maximum_fusion
  30.4 1.0 dynamic-slice_bitcast_fusion
  31.4 1.9 collective-permute-start
  33.3 2.2 %copy.50 = bf16[4,2,448,128]{3,2,0,1:T(8,128)(2,1)} copy(bf16[4,2,448,128]{3,2,1,0:T(8,128)(2,1)} %bitcast.71) | data formatting | bytes 1835008 | tf_op jit(solution)/shard_map/reshape;squeeze | solution.py:74
  35.5 32.3 %all-to-all-done = bf16[128,2,2688]{2,1,0:T(2,128)(2,1)S(1)} async-done(((bf16[128,2,2688]{2,1,0:T(2,128)(2,1)}), bf16[128,2,2688]{2,1,0:T(2,128)(2,1)S(1)}, u32[]{:S(2)}, u32[]{:S(2)}) %all-to-all-start) | async-done | bytes 1376288 | tf_op jit(solution)/shard_map/all_to_all | solution.py:99
  67.8 12.7 %all-to-all-start.2 = ((bf16[8,448,128]{2,1,0:T(8,128)(2,1)}), bf16[8,448,128]{2,1,0:T(8,128)(2,1)}, u32[]{:S(2)}, u32[]{:S(2)}) async-start(bf16[8,448,128]{2,1,0:T(8,128)(2,1)} %bitcast.67), calls=%async_computation.2 | async-start | bytes 1835008 | tf_op jit(solution)/shard_map/all_to_all | solution.py:75
  80.5 2.1 %slice_bitcast_fusion.1 = (bf16[1792,128]{1,0:T(8,128)(2,1)}, bf16[1792,128]{1,0:T(8,128)(2,1)}) fusion(bf16[2,1792,128]{2,1,0:T(8,128)(2,1)} %collective-permute-done), kind=kLoop, calls=%fused_computation.30 | loop fusion | bytes 1835008 | tf_op jit(solution)/shard_map/squeeze | solution.py:107
  82.7 3.0 %copy.48 = bf16[128,2,2688]{0,2,1:T(8,128)(2,1)} copy(bf16[128,2,2688]{2,1,0:T(2,128)(2,1)S(1)} %all-to-all-done) | data formatting | bytes 2752512 | tf_op jit(solution)/shard_map/all_to_all | solution.py:99
  85.7 3.9 %copy.49 = bf16[128,3,2,896]{3,2,1,0:T(2,128)(2,1)S(1)} copy(bf16[128,3,2,896]{0,3,1,2:T(8,128)(2,1)} %bitcast.65) | data formatting | bytes 2752512 | tf_op jit(solution)/shard_map/transpose | solution.py:103
  89.8 0.8 copy-done.1
  91.3 3.9 %collective-permute-start.1 = (bf16[384,256]{1,0:T(8,128)(2,1)S(1)}, bf16[384,256]{1,0:T(8,128)(2,1)S(1)}, u32[]{:S(2)}, u32[]{:S(2)}) collective-permute-start(bf16[384,256]{1,0:T(8,128)(2,1)S(1)} %convolution_convert_fusion.1), channel_id=1, source_target_pairs={{0,2},{2,0},{4,6},{6,4},{8,10},{10,8},{12,14},{14,12},{1,3},{3,1},... | collective-permute-start | bytes 589832 | tf_op jit(solution)/shard_map/ppermute | solution.py:42
  95.3 10.9 %collective-permute-done.1 = bf16[384,256]{1,0:T(8,128)(2,1)S(1)} collective-permute-done((bf16[384,256]{1,0:T(8,128)(2,1)S(1)}, bf16[384,256]{1,0:T(8,128)(2,1)S(1)}, u32[]{:S(2)}, u32[]{:S(2)}) %collective-permute-start.1) | collective-permute-done | bytes 196640 | tf_op jit(solution)/shard_map/ppermute | solution.py:42
  106.7 3.4 %collective-permute-start.2 = (bf16[384,256]{1,0:T(8,128)(2,1)S(1)}, bf16[384,256]{1,0:T(8,128)(2,1)S(1)}, u32[]{:S(2)}, u32[]{:S(2)}) collective-permute-start(bf16[384,256]{1,0:T(8,128)(2,1)S(1)} %get-tuple-element.10), channel_id=1, source_target_pairs={{0,1},{1,0},{2,3},{3,2},{4,5},{5,4},{6,7},{7,6},{8,9},{9,8},{10,11... | collective-permute-start | bytes 589832 | tf_op jit(solution)/shard_map/ppermute | solution.py:42
  110.1 10.8 %collective-permute-done.2 = bf16[384,256]{1,0:T(8,128)(2,1)S(1)} collective-permute-done((bf16[384,256]{1,0:T(8,128)(2,1)S(1)}, bf16[384,256]{1,0:T(8,128)(2,1)S(1)}, u32[]{:S(2)}, u32[]{:S(2)}) %collective-permute-start.2) | collective-permute-done | bytes 196640 | tf_op jit(solution)/shard_map/ppermute | solution.py:42
  121.2 29.9 %all_to_all.20 = bf16[8,384,128]{2,1,0:T(8,128)(2,1)S(1)} all-to-all(bf16[8,384,128]{2,1,0:T(8,128)(2,1)S(1)} %broadcast_in_dim.22), channel_id=1, replica_groups=mesh['expert_0'=8,'expert_1'=4,'expert_2'=2,'section'=8,'tensor'=2] {'se..., dimensions={0} | all-to-all | bytes 1572864 | tf_op jit(solution)/shard_map/all_to_all | solution.py:116
  151.1 1.8 fusion.3
  153.2 1.0 reshape.88
  154.2 6.9 %all-to-all-start.3 = ((bf16[128,3,448]{2,1,0:T(4,128)(2,1)}), bf16[128,3,448]{2,1,0:T(4,128)(2,1)S(1)}, u32[]{:S(2)}, u32[]{:S(2)}) async-start(bf16[128,3,448]{2,1,0:T(4,128)(2,1)} %reshape.88), calls=%async_computation.3 | async-start | bytes 1048576 | tf_op jit(solution)/shard_map/all_to_all | solution.py:123
  161.2 2.6 %fusion.5 = f32[8,16,384]{2,1,0:T(8,128)S(1)} fusion(bf16[8,16,576]{2,1,0:T(8,128)(2,1)S(1)} %copy-done, bf16[8,384,576]{1,2,0:T(8,128)(2,1)} %param.18, pred[8,384]{1,0:T(8,128)(4,1)S(1)} %iota_compare_fusion.2), kind=kOutput, calls=%fused_computation.11 | convolution fusion | flops 56721408 | bytes 3886080 | tf_op jit(solution)/shard_map/rhc,rlc->rhl/dot_general | solution.py:25
  163.9 18.0 %all-to-all-done.3 = bf16[128,3,448]{2,1,0:T(4,128)(2,1)S(1)} async-done(((bf16[128,3,448]{2,1,0:T(4,128)(2,1)}), bf16[128,3,448]{2,1,0:T(4,128)(2,1)S(1)}, u32[]{:S(2)}, u32[]{:S(2)}) %all-to-all-start.3) | async-done | bytes 344096 | tf_op jit(solution)/shard_map/all_to_all | solution.py:123
  182.5 2.5 %collective-permute-start.3 = (f32[16,448]{1,0:T(8,128)S(1)}, f32[16,448]{1,0:T(8,128)S(1)}, u32[]{:S(2)}, u32[]{:S(2)}) collective-permute-start(f32[16,448]{1,0:T(8,128)S(1)} %get-tuple-element.9), channel_id=1, source_target_pairs={{0,8},{2,10},{4,12},{6,14},{8,0},{10,2},{12,4},{14,6},{1,9},{3,11}... | collective-permute-start | bytes 86024 | tf_op jit(solution)/shard_map/ppermute | solution.py:42
  185.0 3.5 %fusion.7 = bf16[8,16,512]{2,1,0:T(8,128)(2,1)} fusion(bf16[8,384,576]{1,2,0:T(8,128)(2,1)} %param.18, f32[8,16]{1,0:T(8,128)S(1)} %fusion.35, f32[8,16,384]{2,1,0:T(8,128)S(1)} %fusion.5), kind=kOutput, calls=%fused_computation.13 | convolution fusion | flops 50545152 | bytes 3674112 | tf_op jit(solution)/shard_map/rhl,rlc->rhc/dot_general | solution.py:35
  188.5 3.8 %collective-permute-done.3 = f32[16,448]{1,0:T(8,128)S(1)} collective-permute-done((f32[16,448]{1,0:T(8,128)S(1)}, f32[16,448]{1,0:T(8,128)S(1)}, u32[]{:S(2)}, u32[]{:S(2)}) %collective-permute-start.3) | collective-permute-done | bytes 28704 | tf_op jit(solution)/shard_map/ppermute | solution.py:42
  192.3 1.4 fusion.28
  (35 shorter events, 4.4 us)
Async XLA Ops:
  0.6 160.5 %copy-start = (bf16[8,16,576]{2,1,0:T(8,128)(2,1)S(1)}, bf16[8,16,576]{2,1,0:T(8,128)(2,1)}, u32[]{:S(2)}) copy-start(bf16[8,16,576]{2,1,0:T(8,128)(2,1)} %param.17) | copy-start | bytes 442372
  0.6 4.4 %copy-start.3 = (f32[16,8]{0,1:T(8,128)S(1)}, f32[16,8]{0,1:T(8,128)}, u32[]{:S(2)}) copy-start(f32[16,8]{0,1:T(8,128)} %param.13) | copy-start | bytes 1540
  10.6 57.2 %all-to-all-start = ((bf16[128,2,2688]{2,1,0:T(2,128)(2,1)}), bf16[128,2,2688]{2,1,0:T(2,128)(2,1)S(1)}, u32[]{:S(2)}, u32[]{:S(2)}) async-start(bf16[128,2,2688]{2,1,0:T(2,128)(2,1)} %copy.47), calls=%async_computation | async-start | bytes 2752512 | tf_op jit(solution)/shard_map/all_to_all | solution.py:99
  31.4 49.1 %collective-permute-start = (bf16[2,1792,128]{2,1,0:T(8,128)(2,1)}, bf16[2,1792,128]{2,1,0:T(8,128)(2,1)}, u32[]{:S(2)}, u32[]{:S(2)}) collective-permute-start(bf16[2,1792,128]{2,1,0:T(8,128)(2,1)} %dynamic-slice_bitcast_fusion), channel_id=1, source_target_pairs={{0,2},{2,0},{4,6},{6,4},{8,10},{10,8},{12,14},{14,12},{1,3},{3,1},... | collective-permute-start | bytes 2752520 | tf_op jit(solution)/shard_map/ppermute | solution.py:42
  67.8 53.2 %all-to-all-start.2 = ((bf16[8,448,128]{2,1,0:T(8,128)(2,1)}), bf16[8,448,128]{2,1,0:T(8,128)(2,1)}, u32[]{:S(2)}, u32[]{:S(2)}) async-start(bf16[8,448,128]{2,1,0:T(8,128)(2,1)} %bitcast.67), calls=%async_computation.2 | async-start | bytes 1835008 | tf_op jit(solution)/shard_map/all_to_all | solution.py:75
  89.6 1.0 copy-start.1
  89.6 1.1 copy-start.2
  91.3 14.9 %collective-permute-start.1 = (bf16[384,256]{1,0:T(8,128)(2,1)S(1)}, bf16[384,256]{1,0:T(8,128)(2,1)S(1)}, u32[]{:S(2)}, u32[]{:S(2)}) collective-permute-start(bf16[384,256]{1,0:T(8,128)(2,1)S(1)} %convolution_convert_fusion.1), channel_id=1, source_target_pairs={{0,2},{2,0},{4,6},{6,4},{8,10},{10,8},{12,14},{14,12},{1,3},{3,1},... | collective-permute-start | bytes 589832 | tf_op jit(solution)/shard_map/ppermute | solution.py:42
  106.7 14.2 %collective-permute-start.2 = (bf16[384,256]{1,0:T(8,128)(2,1)S(1)}, bf16[384,256]{1,0:T(8,128)(2,1)S(1)}, u32[]{:S(2)}, u32[]{:S(2)}) collective-permute-start(bf16[384,256]{1,0:T(8,128)(2,1)S(1)} %get-tuple-element.10), channel_id=1, source_target_pairs={{0,1},{1,0},{2,3},{3,2},{4,5},{5,4},{6,7},{7,6},{8,9},{9,8},{10,11... | collective-permute-start | bytes 589832 | tf_op jit(solution)/shard_map/ppermute | solution.py:42
  153.0 8.1 %copy-start.4 = (s32[8]{0:T(128)S(1)}, s32[8]{0:T(128)}, u32[]{:S(2)}) copy-start(s32[8]{0:T(128)} %param.19) | copy-start | bytes 100
  154.2 27.8 %all-to-all-start.3 = ((bf16[128,3,448]{2,1,0:T(4,128)(2,1)}), bf16[128,3,448]{2,1,0:T(4,128)(2,1)S(1)}, u32[]{:S(2)}, u32[]{:S(2)}) async-start(bf16[128,3,448]{2,1,0:T(4,128)(2,1)} %reshape.88), calls=%async_computation.3 | async-start | bytes 1048576 | tf_op jit(solution)/shard_map/all_to_all | solution.py:123
  182.5 9.8 %collective-permute-start.3 = (f32[16,448]{1,0:T(8,128)S(1)}, f32[16,448]{1,0:T(8,128)S(1)}, u32[]{:S(2)}, u32[]{:S(2)}) collective-permute-start(f32[16,448]{1,0:T(8,128)S(1)} %get-tuple-element.9), channel_id=1, source_target_pairs={{0,8},{2,10},{4,12},{6,14},{8,0},{10,2},{12,4},{14,6},{1,9},{3,11}... | collective-permute-start | bytes 86024 | tf_op jit(solution)/shard_map/ppermute | solution.py:42
